TPU v7x, 32 devices: a whole 2x2x4 slice. The times are simulated.
32 devices in a mesh: dp: 8 (over z, x), shard: 4 (over y, core).
Axes of the slice: x: 2, y: 2, z: 4, core: 2. Of those that a mesh axis runs over, the one named last changes fastest.
Arguments:
- noisy: float32 [128, 256, 16], P(('dp', 'shard')), may hold values from -6 to 6
- velocity: float32 [128, 256, 16], P(('dp', 'shard')), may hold values from -6 to 6
- tstep_idx: int32 [128], P(('dp', 'shard')), may hold values from 0 to 999
- class_ids: int32 [128], P(('dp', 'shard')), may hold values from 0 to 1000
- time_weight: float32 [128], P(('dp', 'shard')), may hold values from 0.3 to 3
- dino: bfloat16 [128, 256, 768], P(('dp', 'shard')), may hold values from -6 to 6
- owner_map: int32 [12], replicated, may hold values from 0 to 11, each once
- adam_flat: float32 [2129920], P(('dp', 'shard')), may hold values from -4 to 4
- adam_m: float32 [2129920], P(('dp', 'shard')), may hold values from -0.015625 to 0.015625
- adam_v: float32 [2129920], P(('dp', 'shard')), may hold values from 1e-06 to 0.0001
- blocks_w: float32 [12, 384, 384], P('shard'), may hold values from -0.3125 to 0.3125
- stat_left: float32 [12, 384, 384], P('shard'), may hold values from -0.005 to 0.01, as said below
- stat_right: float32 [12, 384, 384], P('shard'), may hold values from -0.005 to 0.01, as said below
- root_left: float32 [12, 384, 384], P('shard'), may hold values from -3 to 3, as said below
- root_right: float32 [12, 384, 384], P('shard'), may hold values from -3 to 3, as said below
Outputs:
- loss: float32 [], replicated
- block_update: float32 [12, 384, 384], P('shard')
- stat_left_new: float32 [12, 384, 384], P('shard')
- stat_right_new: float32 [12, 384, 384], P('shard')
- adam_update: float32 [2129920], P(('dp', 'shard'))
- adam_m_new: float32 [2129920], P(('dp', 'shard'))
- adam_v_new: float32 [2129920], P(('dp', 'shard'))
Inputs may be any that keep to these rules, and one draw needn't show every extreme that they name: `owner_map`: each block number appears once. `stat_left`: each slot is symmetric positive definite. `stat_right`: each slot is symmetric positive definite. `root_left`: each slot is symmetric positive definite. `root_right`: each slot is symmetric positive definite.
All inputs are finite; a program needn't handle non-finite values.
Results may differ from a plain program's by a relative error of at most 0.0097.
Values may be sent and summed in bfloat16 or wider, within the bound.
No kernel may reach another device: no remote copies, remote signals or barrier semaphores. Data moves between devices by JAX's collectives and lax.ppermute only.
A program may use at most 192 MiB of HBM per device.

v0:
```python
import functools
import math
import jax
import jax.numpy as jnp
from jax import lax
from jax.sharding import PartitionSpec as P

D = 384
HEADS = 6
HDIM = 64
F = 1536
PD = 16
GRID = 16
SEQ = 256
FREQ = 256
NCLS = 1001
DINO = 768
STEP = 10
NBLK = 12
ADAM_LEN = 2125072
ADAM_PAD = 2129920
HIGHEST = lax.Precision.HIGHEST
BETA_ONE = 0.9
BETA_TWO = 0.95
ADAM_EPS = 1e-08
ADAM_RATE = 0.01
DECAY_RATE = 0.1
STAT_BETA = 0.9
SHAMPOO_RATE = 0.02
RMS_EPS = 1e-08
REPA_WEIGHT = 0.5
NORM_EPS = 1e-06


def segment_shapes():
    return [
        (PD, D),
        (D,),
        (FREQ, D),
        (D,),
        (D, D),
        (D,),
        (NCLS, D),
        (D, 6 * D),
        (6 * D,),
        (D,),
        (D,),
        (D,),
        (F,),
        (D,),
        (D, 2 * D),
        (2 * D,),
        (D, PD),
        (PD,),
        (D, DINO),
        (DINO,),
    ]


def unflatten(flat):
    pieces = []
    offset = 0
    for seg_dims in segment_shapes():
        length = math.prod(seg_dims)
        pieces.append(flat[offset : offset + length].reshape(seg_dims))
        offset += length
    return pieces


def position_table():
    quarter = D // 4
    frequencies = 1.0 / 10000.0 ** (jnp.arange(quarter, dtype=jnp.float32) / quarter)
    cell_ids = jnp.arange(SEQ, dtype=jnp.int32)
    row_arg = (cell_ids // GRID).astype(jnp.float32)[:, None] * frequencies[None, :]
    col_arg = (cell_ids % GRID).astype(jnp.float32)[:, None] * frequencies[None, :]
    return jnp.concatenate(
        [jnp.sin(col_arg), jnp.cos(col_arg), jnp.sin(row_arg), jnp.cos(row_arg)], axis=1
    )


def time_features(tstep_idx):
    half_freq = FREQ // 2
    frequencies = jnp.exp(-math.log(10000.0) * jnp.arange(half_freq, dtype=jnp.float32) / half_freq)
    angles = (tstep_idx.astype(jnp.float32) + 0.5)[:, None] * frequencies[None, :]
    return jnp.concatenate([jnp.cos(angles), jnp.sin(angles)], axis=1)


def normalize(values):
    centered = values - jnp.mean(values, axis=-1, keepdims=True)
    inv_dev = lax.rsqrt(jnp.mean(centered * centered, axis=-1, keepdims=True) + NORM_EPS)
    return (centered * inv_dev, inv_dev)


def normalize_back(grad_in, normed, inv_dev):
    return inv_dev * (
        grad_in
        - jnp.mean(grad_in, axis=-1, keepdims=True)
        - normed * jnp.mean(grad_in * normed, axis=-1, keepdims=True)
    )


def condition_terms(
    tstep_idx,
    class_ids,
    time_in_weight,
    time_in_bias,
    time_out_weight,
    time_out_bias,
    class_table,
    mod_weight,
    mod_bias,
    final_mod_weight,
    final_mod_bias,
):
    features = time_features(tstep_idx)
    time_hidden = jax.nn.silu(jnp.dot(features, time_in_weight, precision=HIGHEST) + time_in_bias)
    onehot_class = (class_ids[:, None] == jnp.arange(NCLS, dtype=jnp.int32)[None, :]).astype(
        jnp.float32
    )
    condition = (
        jnp.dot(time_hidden, time_out_weight, precision=HIGHEST)
        + time_out_bias
        + jnp.dot(onehot_class, class_table, precision=HIGHEST)
    )
    cond_act = jax.nn.silu(condition)
    modulation = jnp.dot(cond_act, mod_weight, precision=HIGHEST) + mod_bias
    final_mods = jnp.dot(cond_act, final_mod_weight, precision=HIGHEST) + final_mod_bias
    return (modulation, final_mods)


def cosine_total(aligned, dino_f):
    products = jnp.sum(aligned * dino_f, axis=-1)
    return jnp.sum(
        products
        * lax.rsqrt(jnp.sum(aligned * aligned, axis=-1) + NORM_EPS)
        * lax.rsqrt(jnp.sum(dino_f * dino_f, axis=-1) + NORM_EPS)
    )


def matmul(left, right):
    return jnp.dot(left, right, preferred_element_type=jnp.float32)


def row_total(rounded):
    return jnp.sum(rounded.astype(jnp.float32), axis=0)


def body(
    noisy,
    velocity,
    tstep_idx,
    class_ids,
    time_weight,
    dino,
    owner_map,
    adam_flat,
    adam_m,
    adam_v,
    blocks_w,
    stat_left,
    stat_right,
    root_left,
    root_right,
):
    devices = lax.axis_size("dp") * lax.axis_size("shard")
    images = noisy.shape[0]
    seq = noisy.shape[1]
    total_img = images * devices
    rows = images * seq
    fc_ratio = F // D
    flat_low = lax.all_gather(adam_flat.astype(jnp.bfloat16), ("dp", "shard"), axis=0, tiled=True)
    slot_low = lax.all_gather(blocks_w.astype(jnp.bfloat16), "shard", axis=0, tiled=True)
    block_ids = jnp.arange(NBLK, dtype=jnp.int32)
    slot_of = jnp.sum(
        block_ids[:, None] * (owner_map[:, None] == block_ids[None, :]).astype(jnp.int32), axis=0
    )
    blocks = jnp.take(slot_low, slot_of, axis=0)
    w_qkv = jnp.concatenate([blocks[0], blocks[1], blocks[2]], axis=1)
    w_proj = blocks[3]
    w_up = jnp.concatenate([blocks[4 + which] for which in range(fc_ratio)], axis=1)
    w_down = blocks[4 + fc_ratio :].reshape(F, D)
    pieces_low = unflatten(flat_low)
    pieces = [piece.astype(jnp.float32) for piece in pieces_low]
    (
        patch_weight,
        patch_bias,
        time_in_weight,
        time_in_bias,
        time_out_weight,
        time_out_bias,
        class_table,
        mod_weight,
        mod_bias,
        query_bias,
        value_bias,
        proj_bias,
        hidden_bias,
        down_bias,
        final_mod_weight,
        final_mod_bias,
        final_weight,
        final_bias,
        align_weight,
        align_bias,
    ) = pieces
    patch_low = pieces_low[0]
    final_low = pieces_low[16]
    align_low = pieces_low[18]
    cond_weights = (
        time_in_weight,
        time_in_bias,
        time_out_weight,
        time_out_bias,
        class_table,
        mod_weight,
        mod_bias,
        final_mod_weight,
        final_mod_bias,
    )
    (modulation, final_mods), cond_back = jax.vjp(
        functools.partial(condition_terms, tstep_idx, class_ids), *cond_weights
    )
    shift_one, scale_one, gate_one, shift_two, scale_two, gate_two = [
        modulation[:, None, which * D : (which + 1) * D] for which in range(6)
    ]
    final_shift = final_mods[:, None, :D]
    final_scale = final_mods[:, None, D:]
    noisy_low = noisy.astype(jnp.bfloat16).reshape(rows, PD)
    hidden0 = (matmul(noisy_low, patch_low) + patch_bias).reshape(images, seq, D) + position_table()
    norm_one, inv_one = normalize(hidden0)
    act_one = (norm_one * (1.0 + scale_one) + shift_one).astype(jnp.bfloat16).reshape(rows, D)
    qkv_bias = jnp.concatenate([query_bias, jnp.zeros((D,), jnp.float32), value_bias])
    projected = (
        (matmul(act_one, w_qkv) + qkv_bias)
        .astype(jnp.bfloat16)
        .reshape(images, seq, 3, HEADS, HDIM)
    )
    queries = projected[:, :, 0]
    key_part = projected[:, :, 1]
    values = projected[:, :, 2]
    scale_qk = HDIM ** (-0.5)
    scores = (
        jnp.einsum("gqhe,gkhe->ghqk", queries, key_part, preferred_element_type=jnp.float32)
        * scale_qk
    )
    row_max = jnp.max(scores, axis=-1, keepdims=True)
    log_total = row_max + jnp.log(jnp.sum(jnp.exp(scores - row_max), axis=-1, keepdims=True))
    probs_low = jnp.exp(scores - log_total).astype(jnp.bfloat16)
    attended = (
        jnp.einsum("ghqk,gkhe->gqhe", probs_low, values, preferred_element_type=jnp.float32)
        .reshape(rows, D)
        .astype(jnp.bfloat16)
    )
    branch_one = (matmul(attended, w_proj) + proj_bias).reshape(images, seq, D)
    hidden1 = hidden0 + gate_one * branch_one
    norm_two, inv_two = normalize(hidden1)
    act_two = (norm_two * (1.0 + scale_two) + shift_two).astype(jnp.bfloat16).reshape(rows, D)
    inner_pre = matmul(act_two, w_up) + hidden_bias
    gelu_out, gelu_back = jax.vjp(functools.partial(jax.nn.gelu, approximate=True), inner_pre)
    gelu_low = gelu_out.astype(jnp.bfloat16)
    branch_two = (matmul(gelu_low, w_down) + down_bias).reshape(images, seq, D)
    hidden2 = hidden1 + gate_two * branch_two
    norm_three, inv_three = normalize(hidden2)
    act_three = (
        (norm_three * (1.0 + final_scale) + final_shift).astype(jnp.bfloat16).reshape(rows, D)
    )
    output = (matmul(act_three, final_low) + final_bias).reshape(images, seq, PD)
    errors = output - velocity
    main_term = jnp.sum(time_weight[:, None, None] * errors * errors) / (total_img * SEQ * PD)
    hidden1_low = hidden1.astype(jnp.bfloat16).reshape(rows, D)
    aligned = matmul(hidden1_low, align_low) + align_bias
    dino_f = dino.astype(jnp.float32).reshape(rows, DINO)
    cosine_sum, cosine_back = jax.vjp(functools.partial(cosine_total, dino_f=dino_f), aligned)
    align_scale = REPA_WEIGHT / (total_img * SEQ)
    loss_local = main_term - align_scale * cosine_sum
    back_output = (
        (2.0 * time_weight[:, None, None] * errors / (total_img * SEQ * PD))
        .reshape(rows, PD)
        .astype(jnp.bfloat16)
    )
    grad_final = matmul(act_three.T, back_output)
    grad_final_bias = row_total(back_output)
    back_three = matmul(back_output, final_low.T).reshape(images, seq, D)
    grad_final_shift = jnp.sum(back_three, axis=1)
    grad_final_scale = jnp.sum(back_three * norm_three, axis=1)
    back_hidden2 = normalize_back(back_three * (1.0 + final_scale), norm_three, inv_three)
    back_branch_two = (back_hidden2 * gate_two).reshape(rows, D).astype(jnp.bfloat16)
    grad_gate_two = jnp.sum(back_hidden2 * branch_two, axis=1)
    grad_down = matmul(gelu_low.T, back_branch_two)
    grad_down_bias = row_total(back_branch_two)
    back_inner = gelu_back(matmul(back_branch_two, w_down.T))[0].astype(jnp.bfloat16)
    grad_up = matmul(act_two.T, back_inner)
    grad_hidden_bias = row_total(back_inner)
    back_two = matmul(back_inner, w_up.T).reshape(images, seq, D)
    grad_shift_two = jnp.sum(back_two, axis=1)
    grad_scale_two = jnp.sum(back_two * norm_two, axis=1)
    back_aligned = cosine_back(jnp.asarray(-align_scale, jnp.float32))[0].astype(jnp.bfloat16)
    grad_align = matmul(hidden1_low.T, back_aligned)
    grad_align_bias = row_total(back_aligned)
    back_hidden1 = (
        back_hidden2
        + normalize_back(back_two * (1.0 + scale_two), norm_two, inv_two)
        + matmul(back_aligned, align_low.T).reshape(images, seq, D)
    )
    back_branch_one = (back_hidden1 * gate_one).reshape(rows, D).astype(jnp.bfloat16)
    grad_gate_one = jnp.sum(back_hidden1 * branch_one, axis=1)
    grad_proj = matmul(attended.T, back_branch_one)
    grad_proj_bias = row_total(back_branch_one)
    back_attended = (
        matmul(back_branch_one, w_proj.T).astype(jnp.bfloat16).reshape(images, seq, HEADS, HDIM)
    )
    back_probs = jnp.einsum(
        "gqhe,gkhe->ghqk", back_attended, values, preferred_element_type=jnp.float32
    )
    grad_values = jnp.einsum(
        "ghqk,gqhe->gkhe", probs_low, back_attended, preferred_element_type=jnp.float32
    )
    scores_again = (
        jnp.einsum("gqhe,gkhe->ghqk", queries, key_part, preferred_element_type=jnp.float32)
        * scale_qk
    )
    probs_again = jnp.exp(scores_again - log_total)
    back_scores = (
        probs_again * (back_probs - jnp.sum(back_probs * probs_again, axis=-1, keepdims=True))
    ).astype(jnp.bfloat16)
    grad_queries = (
        jnp.einsum("ghqk,gkhe->gqhe", back_scores, key_part, preferred_element_type=jnp.float32)
        * scale_qk
    )
    grad_keys = (
        jnp.einsum("ghqk,gqhe->gkhe", back_scores, queries, preferred_element_type=jnp.float32)
        * scale_qk
    )
    back_projected = (
        jnp.stack([grad_queries, grad_keys, grad_values], axis=2)
        .reshape(rows, 3 * D)
        .astype(jnp.bfloat16)
    )
    grad_qkv = matmul(act_one.T, back_projected)
    grad_qkv_bias = row_total(back_projected)
    back_one = matmul(back_projected, w_qkv.T).reshape(images, seq, D)
    grad_shift_one = jnp.sum(back_one, axis=1)
    grad_scale_one = jnp.sum(back_one * norm_one, axis=1)
    back_hidden0 = (
        (back_hidden1 + normalize_back(back_one * (1.0 + scale_one), norm_one, inv_one))
        .reshape(rows, D)
        .astype(jnp.bfloat16)
    )
    grad_patch = matmul(noisy_low.T, back_hidden0)
    grad_patch_bias = row_total(back_hidden0)
    grad_modulation = jnp.concatenate(
        [
            grad_shift_one,
            grad_scale_one,
            grad_gate_one,
            grad_shift_two,
            grad_scale_two,
            grad_gate_two,
        ],
        axis=1,
    )
    grad_final_mods = jnp.concatenate([grad_final_shift, grad_final_scale], axis=1)
    cond_grads = cond_back((grad_modulation, grad_final_mods))
    grad_list = (
        [grad_patch, grad_patch_bias]
        + list(cond_grads[:7])
        + [
            grad_qkv_bias[:D],
            grad_qkv_bias[2 * D :],
            grad_proj_bias,
            grad_hidden_bias,
            grad_down_bias,
            cond_grads[7],
            cond_grads[8],
            grad_final,
            grad_final_bias,
            grad_align,
            grad_align_bias,
        ]
    )
    flat_grad = jnp.concatenate(
        [gradient_part.reshape(-1) for gradient_part in grad_list]
        + [jnp.zeros((ADAM_PAD - ADAM_LEN,), jnp.float32)]
    )
    grad_model = jnp.concatenate(
        [
            grad_qkv.reshape(D, 3, D).transpose(1, 0, 2),
            grad_proj[None],
            grad_up.reshape(D, fc_ratio, D).transpose(1, 0, 2),
            grad_down.reshape(fc_ratio, D, D),
        ],
        axis=0,
    )
    grad_slot = jnp.take(grad_model, owner_map, axis=0)
    flat_owned = lax.psum_scatter(flat_grad, ("dp", "shard"), scatter_dimension=0, tiled=True)
    loss_total = lax.psum(loss_local, ("dp", "shard"))
    summed = lax.psum(grad_slot, "dp")
    owned = lax.psum_scatter(
        summed.astype(jnp.bfloat16), "shard", scatter_dimension=0, tiled=True
    ).astype(jnp.float32)
    new_left = STAT_BETA * stat_left + (1.0 - STAT_BETA) * jnp.einsum(
        "bij,bkj->bik", owned, owned, precision=HIGHEST
    )
    new_right = STAT_BETA * stat_right + (1.0 - STAT_BETA) * jnp.einsum(
        "bji,bjk->bik", owned, owned, precision=HIGHEST
    )
    left_applied = jnp.einsum("bij,bjk->bik", root_left, owned, precision=HIGHEST)
    direction = jnp.einsum("bij,bjk->bik", left_applied, root_right, precision=HIGHEST)
    root_mean = jnp.sqrt(jnp.mean(direction * direction, axis=(1, 2), keepdims=True))
    block_update = -SHAMPOO_RATE * (direction / (root_mean + RMS_EPS) + DECAY_RATE * blocks_w)
    new_m = BETA_ONE * adam_m + (1.0 - BETA_ONE) * flat_owned
    new_v = BETA_TWO * adam_v + (1.0 - BETA_TWO) * flat_owned * flat_owned
    corrected_m = new_m / (1.0 - BETA_ONE**STEP)
    corrected_v = new_v / (1.0 - BETA_TWO**STEP)
    adam_update = -ADAM_RATE * (
        corrected_m / (jnp.sqrt(corrected_v) + ADAM_EPS) + DECAY_RATE * adam_flat
    )
    return (loss_total, block_update, new_left, new_right, adam_update, new_m, new_v)


def solution(mesh):
    return jax.shard_map(
        body,
        mesh=mesh,
        in_specs=(
            P(("dp", "shard"), None, None),
            P(("dp", "shard"), None, None),
            P(("dp", "shard")),
            P(("dp", "shard")),
            P(("dp", "shard")),
            P(("dp", "shard"), None, None),
            P(),
            P(("dp", "shard")),
            P(("dp", "shard")),
            P(("dp", "shard")),
            P("shard", None, None),
            P("shard", None, None),
            P("shard", None, None),
            P("shard", None, None),
            P("shard", None, None),
        ),
        out_specs=(
            P(),
            P("shard", None, None),
            P("shard", None, None),
            P("shard", None, None),
            P(("dp", "shard")),
            P(("dp", "shard")),
            P(("dp", "shard")),
        ),
        check_vma=False,
    )
```

profile of v0, /device:TPU:0, one launch (start us, length us, event | category | flops | bytes accessed | tf_op | source)
XLA Modules:
  0.0 797.5 jit_solution(3456417252762726016)
XLA Ops:
  7.3 2.6 convert_element_type.209
  17.3 26.3 %all-gather.5.cloned.1.call-done = bf16[12,384,384]{2,1,0:T(8,128)(2,1)} async-done(((bf16[3,384,384]{2,1,0:T(8,128)(2,1)}), bf16[12,384,384]{2,1,0:T(8,128)(2,1)}) %all-gather.5.cloned.1.call-update) | async-done | bytes 3538960 | tf_op jit(solution)/shard_map/all_gather | solution.py:172
  43.6 5.1 gather_fusion
  48.7 2.5 broadcast_select_fusion.1
  54.7 54.4 %all-gather.3.cloned.1.call-done = bf16[2129920]{0:T(1024)(128)(2,1)} async-done(((bf16[66560]{0:T(1024)(128)(2,1)}), bf16[2129920]{0:T(1024)(128)(2,1)}) %all-gather.3.cloned.1.call-update) | async-done | bytes 4259856 | tf_op jit(solution)/shard_map/all_gather | solution.py:171
  122.9 3.3 reshape.435
  137.7 2.9 fusion.19
  140.5 4.3 copy.90
  144.9 6.1 reshape.436
  151.0 2.4 fusion.110
  159.4 3.6 fusion.106
  169.8 3.8 fusion.104
  182.8 2.9 multiply_reduce_fusion.7
  185.8 2.2 convert_reduce_fusion.3
  188.0 7.3 fusion.13
  195.3 5.1 convert_reduce_fusion
  200.5 3.1 fusion.33
  203.7 3.5 multiply_reduce_fusion.2
  210.2 3.0 convert_reduce_fusion.4
  214.0 2.5 convolution_convert_fusion.1
  216.6 2.3 copy.98
  218.8 2.8 reshape.446
  221.7 7.7 multiply_reduce_fusion
  229.4 6.3 multiply_convert_fusion
  239.2 2.2 convolution_bitcast_fusion.2
  241.5 2.2 multiply_reduce_fusion.4
  247.1 2.5 multiply_reduce_fusion.6
  249.7 2.7 convert_reduce_fusion.5
  252.4 4.8 fusion.95
  259.9 2.3 fusion.55
  265.5 3.4 fusion.46
  271.7 3.4 copy.104
  276.5 4.7 reshape.451
  291.9 2.4 reshape.452
  300.5 87.2 %concatenate.35 = f32[2129920]{0:T(1024)} concatenate(f32[6144]{0:T(1024)} %reshape.447, f32[384]{0:T(512)} %get-tuple-element.39, f32[98304]{0:T(1024)S(1)} %copy-done.57, f32[384]{0:T(512)} %get-tuple-element.37, f32[147456]{0:T(1024)S(1)} %reshape.449, f32[384]{0:T(512)} %get-tuple-element.110, f32[384384]{0:T(1024)} %reshape.450, f32[884736]{0:T(1024)} %reshape.451, ...), dimensions={0} | concatenate | bytes 17039360 | tf_op jit(solution)/shard_map/concatenate | solution.py:381
  387.8 2.3 copy.141
  391.3 4.9 copy.131
  396.2 5.1 convolution_bitcast_fusion
  401.3 4.7 copy.132
  406.1 4.2 fusion.114
  410.3 3.3 pad_maximum_fusion
  413.5 7.0 gather_fusion.1
  420.6 6.6 broadcast_select_fusion
  427.1 306.0 %all-reduce.5 = bf16[12,384,384]{2,1,0:T(8,128)(2,1)} all-reduce(f32[12,384,384]{2,1,0:T(8,128)} %broadcast_select_fusion), channel_id=1, replica_groups=mesh['dp'=8,'shard'=4] {'dp'}, use_global_device_ids=true, to_apply=%region_20.21 | all-reduce | flops 1769472 | bytes 10616832 | tf_op jit(solution)/shard_map/psum | solution.py:397
  734.7 40.7 %psum.14 = f32[]{:T(128)} all-reduce(f32[]{:T(128)S(6)} %sub.143), channel_id=1, replica_groups=mesh['dp'=8,'shard'=4] {'dp','shard'}, use_global_device_ids=true, to_apply=%region_14.15 | all-reduce | flops 1 | bytes 8 | tf_op jit(solution)/shard_map/psum | solution.py:396
  775.4 2.2 add_multiply_fusion.1
  777.5 3.0 fusion.115
  780.6 3.8 multiply_reduce_fusion.3
  (344 shorter events, 103.5 us)
Async XLA Ops:
  7.2 773.4 %copy-start = (f32[3,384,384]{2,1,0:T(8,128)S(1)}, f32[3,384,384]{2,1,0:T(8,128)}, u32[]{:S(2)}) copy-start(f32[3,384,384]{2,1,0:T(8,128)} %param.29) | copy-start | bytes 5308420
  7.2 4.5 copy-start.78
  7.2 5.1 copy-start.22
  7.2 36.4 %all-gather.5.cloned.1.call-start = ((), (), s32[]{:S(2)}) async-start(), calls=%async_computation.2 | async-start | bytes 4423680 | tf_op jit(solution)/shard_map/all_gather | solution.py:172
  9.9 99.2 %all-gather.3.cloned.1.call-start = ((), (), s32[]{:S(2)}) async-start(), calls=%async_computation.1 | async-start | bytes 4392960 | tf_op jit(solution)/shard_map/all_gather | solution.py:171
  11.6 5.1 copy-start.98
  11.6 5.1 copy-start.96
  11.6 763.7 %all-reduce.4.cloned.1.call-start = ((), (), s32[]{:S(2)}) async-start(), calls=%async_computation.4 | async-start | bytes 17039360
  17.3 114.4 %copy-start.88 = (f32[4,128]{1,0:T(4,128)}, f32[4,128]{1,0:T(4,128)S(1)}, u32[]{:S(2)}) copy-start(f32[4,128]{1,0:T(4,128)S(1)} %get-tuple-element.90) | copy-start | bytes 6148
  17.3 114.4 %copy-start.90 = (f32[4,128]{1,0:T(4,128)}, f32[4,128]{1,0:T(4,128)S(1)}, u32[]{:S(2)}) copy-start(f32[4,128]{1,0:T(4,128)S(1)} %get-tuple-element.91) | copy-start | bytes 6148
  128.4 3.8 copy-start.48
  130.1 4.8 copy-start.17
  131.7 4.6 copy-start.86
  131.9 4.4 copy-start.8
  136.3 4.3 copy-start.80
  159.1 3.8 copy-start.30
  169.8 3.8 copy-start.13
  169.8 6.8 copy-start.82
  178.0 4.8 copy-start.5
  178.0 4.8 copy-start.10
  178.0 4.8 copy-start.84
  178.0 4.8 copy-start.91
  180.8 7.1 slice-start.2
  182.8 5.2 slice-start.3
  188.0 7.3 copy-start.66
  195.3 5.1 copy-start.3
  195.3 5.1 copy-start.59
  195.3 5.1 copy-start.61
  195.3 5.1 copy-start.63
  195.3 5.1 copy-start.65
  221.7 17.5 %slice-start = ((s8[6291456]{0:T(1024)(128)(4,1)}), s8[4194304]{0:T(1024)(128)(4,1)S(1)}, s32[]{:S(2)}) async-start(s8[6291456]{0:T(1024)(128)(4,1)} %bitcast.283), calls=%async_computation.5 | async-start | bytes 8388608
  229.4 6.4 copy-start.26
  229.4 9.8 %slice-start.1 = ((s8[6291456]{0:T(1024)(128)(4,1)}), s8[2097152]{0:T(1024)(128)(4,1)S(1)}, s32[]{:S(2)}) async-start(s8[6291456]{0:T(1024)(128)(4,1)} %bitcast.283), calls=%async_computation.6 | async-start | bytes 4194304
  252.4 4.8 copy-start.42
  252.4 5.3 copy-start.18
  257.7 6.1 copy-start.50
  257.7 7.7 copy-start.4
  265.5 6.2 copy-start.16
  276.5 4.7 copy-start.40
  282.4 8.4 %copy-start.38 = (f32[384,768]{1,0:T(8,128)S(1)}, f32[384,768]{1,0:T(8,128)}, u32[]{:S(2)}) copy-start(f32[384,768]{1,0:T(8,128)} %fusion.46) | copy-start | bytes 3538948
  291.9 6.4 copy-start.33
  291.9 8.6 %copy-start.57 = (f32[98304]{0:T(1024)S(1)}, f32[98304]{0:T(1024)}, u32[]{:S(2)}) copy-start(f32[98304]{0:T(1024)} %reshape.448) | copy-start | bytes 1179652
  387.7 389.8 %reduce-scatter.2.cloned.1.call-start = ((), (), s32[]{:S(2)}) async-start(), calls=%async_computation.3 | async-start | bytes 4423680 | tf_op jit(solution)/shard_map/reduce_scatter | solution.py:398
  406.1 4.2 copy-start.52
  406.1 4.2 copy-start.53
  413.5 7.0 copy-start.95
  733.2 44.4 %copy-start.54 = (f32[3,384,384]{2,1,0:T(8,128)S(1)}, f32[3,384,384]{2,1,0:T(8,128)}, u32[]{:S(2)}) copy-start(f32[3,384,384]{2,1,0:T(8,128)} %param.28) | copy-start | bytes 5308420
  780.6 3.8 copy-start.29
  (59 other events, 135.7 us)
Sparse Core Ops, SparseCore 0:
  10.1 33.4 all-gather.4
  47.1 61.9 all-gather.2
  387.8 243.0 all-reduce.3
  733.3 39.5 reduce-scatter.1
where the time goes:
time: 810 us; the launch traced here: 798 us
  blocking collectives  347 us (43%)
  local copies, waits for them, and re-layouts  186 us (23%)
  matrix products  103 us (13%)
  waiting for transfers between devices  80.8 us (10%)
  other arithmetic  64.9 us (8%)
  between operations  16.6 us (2%)
    psum x1, blocking collectives, body(): summed = lax.psum(grad_slot, 'dp')  306 us
    concatenate x1, local copies, waits for them, and re-layouts, body(): jnp.concatenate([gradient_part.reshape(-1) for gradient_part in grad_list...  87.2 us
    dot_general x20, matrix products, matmul(): return jnp.dot(left, right, preferred_element_type=jnp.float32)  57.1 us
    all_gather x1, waiting for transfers between devices, body(): lax.all_gather(adam_flat.astype(jnp.bfloat16), ('dp', 'shard'), axis=0, t...  54.4 us
    psum x1, blocking collectives, body(): loss_total = lax.psum(loss_local, ('dp', 'shard'))  40.7 us
    all_gather x1, waiting for transfers between devices, body(): lax.all_gather(blocks_w.astype(jnp.bfloat16), 'shard', axis=0, tiled=True)  26.3 us
  transfers between devices with their start and end apart: 4, of which 2 were waited for; matrix products, arithmetic and copies ran while one was open for 7% of the time, Pallas kernels for 0%

commit v1 on v0

--- a/solution.py
+++ b/solution.py
@@ -4,6 +4,7 @@
 import jax.numpy as jnp
 from jax import lax
 from jax.sharding import PartitionSpec as P
+from jax.lax import all_gather
 
 D = 384
 HEADS = 6
@@ -394,7 +395,7 @@
     grad_slot = jnp.take(grad_model, owner_map, axis=0)
     flat_owned = lax.psum_scatter(flat_grad, ("dp", "shard"), scatter_dimension=0, tiled=True)
     loss_total = lax.psum(loss_local, ("dp", "shard"))
-    summed = lax.psum(grad_slot, "dp")
+    summed = jnp.sum(all_gather(grad_slot, axis_name="dp"), axis=0)
     owned = lax.psum_scatter(
         summed.astype(jnp.bfloat16), "shard", scatter_dimension=0, tiled=True
     ).astype(jnp.float32)

time: 810 us -> 1610 us (1.99)
  waiting for transfers between devices: 80.8 us -> 1170 us
  blocking collectives: 347 us -> 40.9 us
  other arithmetic: 64.9 us -> 84.3 us
    all_gather x0 -> x1, waiting for transfers between devices: none -> 923 us  [body(): summed = jnp.sum(all_gather(grad_slot, axis_name='dp'), axis=0)]
    psum x1 -> x0, blocking collectives: 306 us -> none  [body(): summed = lax.psum(grad_slot, 'dp')]
    unnamed x5 -> x6, waiting for transfers between devices: 0.07 us -> 123 us
    reduce_scatter x1, waiting for transfers between devices: 0.01 us -> 40.7 us  [body(): lax.psum_scatter(summed.astype(jnp.bfloat16), 'shard', scatter_dimension=...]
    reduce_sum x0 -> x1, other arithmetic: none -> 22.2 us  [body(): summed = jnp.sum(all_gather(grad_slot, axis_name='dp'), axis=0)]
  transfers between devices with their start and end apart: 4 -> 5, of which waited for: 2 -> 5; matrix products, arithmetic and copies ran while one was open for 7% -> 12% of each run, Pallas kernels for 0% -> 0%
where the time goes in v1:
time: 1610 us; the launch traced here: 1600 us
  waiting for transfers between devices  1170 us (73%)
  local copies, waits for them, and re-layouts  189 us (12%)
  matrix products  103 us (6%)
  other arithmetic  84.3 us (5%)
  blocking collectives  40.9 us (3%)
  between operations  16.8 us (1%)
    all_gather x1, waiting for transfers between devices, body(): summed = jnp.sum(all_gather(grad_slot, axis_name='dp'), axis=0)  923 us
    unnamed x6, waiting for transfers between devices  123 us
    concatenate x1, local copies, waits for them, and re-layouts, body(): jnp.concatenate([gradient_part.reshape(-1) for gradient_part in grad_list...  87.1 us
    dot_general x20, matrix products, matmul(): return jnp.dot(left, right, preferred_element_type=jnp.float32)  60 us
    all_gather x1, waiting for transfers between devices, body(): lax.all_gather(adam_flat.astype(jnp.bfloat16), ('dp', 'shard'), axis=0, t...  54.3 us
    psum x1, blocking collectives, body(): loss_total = lax.psum(loss_local, ('dp', 'shard'))  40.9 us
    reduce_scatter x1, waiting for transfers between devices, body(): lax.psum_scatter(summed.astype(jnp.bfloat16), 'shard', scatter_dimension=...  40.7 us
  transfers between devices with their start and end apart: 5, of which 5 were waited for; matrix products, arithmetic and copies ran while one was open for 12% of the time, Pallas kernels for 0%

profile of v1, /device:TPU:0, one launch (start us, length us, event | category | flops | bytes accessed | tf_op | source)
XLA Modules:
  0.0 1601.4 jit_solution(17345270123690071206)
XLA Ops:
  7.3 2.6 convert_element_type.209
  17.2 26.4 %all-gather.6.cloned.1.call-done = bf16[12,384,384]{2,1,0:T(8,128)(2,1)} async-done(((bf16[3,384,384]{2,1,0:T(8,128)(2,1)}), bf16[12,384,384]{2,1,0:T(8,128)(2,1)}) %all-gather.6.cloned.1.call-update) | async-done | bytes 3538960 | tf_op jit(solution)/shard_map/all_gather | solution.py:173
  43.6 5.1 gather_fusion
  48.7 2.5 broadcast_select_fusion
  54.8 54.3 %all-gather.4.cloned.1.call-done = bf16[2129920]{0:T(1024)(128)(2,1)} async-done(((bf16[66560]{0:T(1024)(128)(2,1)}), bf16[2129920]{0:T(1024)(128)(2,1)}) %all-gather.4.cloned.1.call-update) | async-done | bytes 4259856 | tf_op jit(solution)/shard_map/all_gather | solution.py:172
  122.9 3.3 reshape.442
  137.7 2.9 fusion.19
  140.5 4.3 copy.94
  144.8 6.1 reshape.443
  150.9 2.4 fusion.110
  159.3 3.6 fusion.106
  169.2 3.7 fusion.104
  180.3 3.5 multiply_reduce_fusion.7
  186.0 7.4 fusion.13
  193.4 5.1 convert_reduce_fusion
  198.6 3.1 fusion.33
  201.7 3.4 multiply_reduce_fusion.2
  209.0 3.0 convert_reduce_fusion.4
  212.9 2.5 convolution_convert_fusion.1
  215.4 2.3 copy.102
  217.7 2.8 reshape.453
  220.5 7.6 multiply_reduce_fusion
  228.1 6.5 multiply_convert_fusion
  243.9 2.4 convolution_bitcast_fusion.1
  246.3 5.1 copy.135
  251.4 5.0 convolution_bitcast_fusion
  256.4 4.7 copy.136
  261.0 4.0 fusion.114
  265.1 3.1 pad_maximum_fusion
  268.2 7.0 gather_fusion.1
  275.1 6.5 bitcast_select_fusion
  281.8 3.5 copy.116
  285.3 4.8 multiply_reduce_fusion.6
  290.2 2.5 convert_reduce_fusion.5
  295.7 4.8 fusion.95
  300.5 4.7 reshape.458
  306.9 2.9 fusion.113
  323.7 3.2 fusion.46
  326.9 2.3 reshape.461
  331.4 2.4 reshape.459
  340.7 87.1 %concatenate.35 = f32[2129920]{0:T(1024)} concatenate(f32[6144]{0:T(1024)} %reshape.454, f32[384]{0:T(512)} %get-tuple-element.39, f32[98304]{0:T(1024)S(1)} %copy-done.54, f32[384]{0:T(512)} %get-tuple-element.37, f32[147456]{0:T(1024)S(1)} %copy-done.47, f32[384]{0:T(512)} %get-tuple-element.110, f32[384384]{0:T(1024)} %reshape.457, f32[884736]{0:T(1024)} %reshape.458, ...), dimensions={0} | concatenate | bytes 17039360 | tf_op jit(solution)/shard_map/concatenate | solution.py:382
  427.9 922.9 %all-gather.8.cloned.1.call-done = f32[8,12,384,384]{3,2,1,0:T(8,128)} async-done(((f32[1,12,384,384]{3,2,1,0:T(8,128)}), f32[8,12,384,384]{3,2,1,0:T(8,128)}) %all-gather.8.cloned.1.call-update) | async-done | bytes 56623120 | tf_op jit(solution)/shard_map/all_gather | solution.py:398
  1350.8 22.2 %reduce_sum.406 = bf16[12,384,384]{2,1,0:T(8,128)(2,1)} reduce(f32[8,12,384,384]{3,2,1,0:T(8,128)} %all-gather.8.cloned.1.call-done, f32[]{:T(128)} %constant.126.clone.1), dimensions={0}, to_apply=%region_20.21 | reduce | flops 12386304 | bytes 60162052 | tf_op jit(solution)/shard_map/reduce_sum | solution.py:398
  1374.5 40.9 %psum.7 = f32[]{:T(128)} all-reduce(f32[]{:T(128)S(6)} %sub.143), channel_id=1, replica_groups=mesh['dp'=8,'shard'=4] {'dp','shard'}, use_global_device_ids=true, to_apply=%region_14.15 | all-reduce | flops 1 | bytes 8 | tf_op jit(solution)/shard_map/psum | solution.py:397
  1415.3 123.2 %all-reduce.3.cloned.1.call-done = f32[2129920]{0:T(1024)} async-done(((f32[2129920]{0:T(1024)}), f32[2129920]{0:T(1024)}) %all-reduce.3.cloned.1.call-update) | async-done | bytes 8519696
  1540.7 40.7 %reduce-scatter.2.cloned.1.call-done = bf16[3,384,384]{2,1,0:T(8,128)(2,1)} async-done(((bf16[12,384,384]{2,1,0:T(8,128)(2,1)}), bf16[3,384,384]{2,1,0:T(8,128)(2,1)}) %reduce-scatter.2.cloned.1.call-update) | async-done | bytes 884752 | tf_op jit(solution)/shard_map/reduce_scatter | solution.py:399
  1581.4 3.0 fusion.115
  1584.4 3.8 multiply_reduce_fusion.3
  (357 shorter events, 107.8 us)
Async XLA Ops:
  7.2 1577.2 %copy-start = (f32[3,384,384]{2,1,0:T(8,128)S(1)}, f32[3,384,384]{2,1,0:T(8,128)}, u32[]{:S(2)}) copy-start(f32[3,384,384]{2,1,0:T(8,128)} %param.29) | copy-start | bytes 5308420
  7.2 4.5 copy-start.73
  7.2 5.1 copy-start.23
  7.2 36.4 %all-gather.6.cloned.1.call-start = ((), (), s32[]{:S(2)}) async-start(), calls=%async_computation.2 | async-start | bytes 4423680 | tf_op jit(solution)/shard_map/all_gather | solution.py:173
  9.9 99.2 %all-gather.4.cloned.1.call-start = ((), (), s32[]{:S(2)}) async-start(), calls=%async_computation.1 | async-start | bytes 4392960 | tf_op jit(solution)/shard_map/all_gather | solution.py:172
  11.6 5.0 copy-start.103
  11.6 5.0 copy-start.101
  11.6 1339.2 %all-gather.8.cloned.1.call-start = ((), (), s32[]{:S(2)}) async-start(), calls=%async_computation.3 | async-start | bytes 63700992 | tf_op jit(solution)/shard_map/all_gather | solution.py:398
  17.2 114.4 %copy-start.92 = (f32[4,128]{1,0:T(4,128)}, f32[4,128]{1,0:T(4,128)S(1)}, u32[]{:S(2)}) copy-start(f32[4,128]{1,0:T(4,128)S(1)} %get-tuple-element.90) | copy-start | bytes 6148
  17.2 114.4 %copy-start.94 = (f32[4,128]{1,0:T(4,128)}, f32[4,128]{1,0:T(4,128)S(1)}, u32[]{:S(2)}) copy-start(f32[4,128]{1,0:T(4,128)S(1)} %get-tuple-element.91) | copy-start | bytes 6148
  130.0 4.8 copy-start.16
  131.6 4.6 copy-start.90
  136.3 28.5 %copy-start.81 = (f32[4,384]{1,0:T(4,128)}, f32[4,384]{1,0:T(4,128)S(1)}, u32[]{:S(2)}) copy-start(f32[4,384]{1,0:T(4,128)S(1)} %get-tuple-element.117) | copy-start | bytes 18436
  164.7 42.5 %copy-start.87 = (f32[4,256]{1,0:T(4,128)}, f32[4,256]{1,0:T(4,128)S(1)}, u32[]{:S(2)}) copy-start(f32[4,256]{1,0:T(4,128)S(1)} %rsqrt.60) | copy-start | bytes 12292
  169.2 6.1 copy-start.86
  175.4 4.8 copy-start.96
  175.5 4.8 copy-start.5
  175.5 4.8 copy-start.10
  178.3 7.7 slice-start.2
  180.2 5.8 slice-start.3
  186.0 7.4 copy-start.63
  193.4 5.2 copy-start.3
  193.4 5.2 copy-start.56
  193.4 5.2 copy-start.58
  193.4 5.1 copy-start.60
  193.4 5.1 copy-start.62
  193.4 5.1 copy-start.82
  207.2 4.8 copy-start.22
  220.5 16.4 %slice-start = ((s8[6291456]{0:T(1024)(128)(4,1)}), s8[4194304]{0:T(1024)(128)(4,1)S(1)}, s32[]{:S(2)}) async-start(s8[6291456]{0:T(1024)(128)(4,1)} %bitcast.285), calls=%async_computation.6 | async-start | bytes 8388608
  228.1 6.5 copy-start.28
  228.1 8.8 slice-start.1
  268.2 7.0 copy-start.100
  281.7 1256.8 %all-reduce.3.cloned.1.call-start = ((), (), s32[]{:S(2)}) async-start(), calls=%async_computation.5 | async-start | bytes 17039360
  285.3 4.9 copy-start.7
  285.3 4.9 copy-start.12
  285.3 4.9 copy-start.40
  300.5 6.4 copy-start.17
  305.2 5.2 copy-start.99
  312.8 5.8 copy-start.93
  312.8 5.8 copy-start.95
  312.8 8.9 copy-start.74
  314.5 9.1 copy-start.4
  329.3 9.3 copy-start.33
  331.4 9.3 copy-start.76
  331.4 9.3 copy-start.47
  331.4 9.3 copy-start.54
  427.8 1153.5 %reduce-scatter.2.cloned.1.call-start = ((), (), s32[]{:S(2)}) async-start(), calls=%async_computation.4 | async-start | bytes 4423680 | tf_op jit(solution)/shard_map/reduce_scatter | solution.py:399
  1373.0 208.4 %copy-start.50 = (f32[3,384,384]{2,1,0:T(8,128)S(1)}, f32[3,384,384]{2,1,0:T(8,128)}, u32[]{:S(2)}) copy-start(f32[3,384,384]{2,1,0:T(8,128)} %param.28) | copy-start | bytes 5308420
  (65 other events, 159.6 us)
Sparse Core Ops, SparseCore 0:
  10.1 33.4 all-gather.5
  47.1 61.9 all-gather.3
  281.8 1068.9 all-gather.7
  1356.5 181.9 all-reduce.2
  1540.9 40.4 reduce-scatter.1
